TPU v7x, 32 devices: a whole 2x2x4 slice. The times are simulated.
32 devices in a mesh: ctx: 8 (over z, y), tp: 4 (over x, core).
Axes of the slice: x: 2, y: 2, z: 4, core: 2. Of those that a mesh axis runs over, the one named last changes fastest.
Arguments:
- queries: bfloat16 [4096, 8192], P('ctx', 'tp'), may hold values from -6 to 6
- keys: bfloat16 [4096, 1024], P('ctx', 'tp'), may hold values from -6 to 6
- values: bfloat16 [4096, 1024], P('ctx', 'tp'), may hold values from -6 to 6
- block_plan: int32 [8, 4], replicated, may hold values from 0 to 7, as said below
- doc_lengths: int32 [16], replicated, may hold values from 1 to 2048, 4096 in all
- scan_input: bfloat16 [4096, 16384], P('ctx', 'tp'), may hold values from -6 to 6
- gate_input: bfloat16 [4096, 16384], P('ctx', 'tp'), may hold values from -600 to 600
- step_size: bfloat16 [4096, 256], P('ctx', 'tp'), may hold values from 0 to 6
- decay_rate: float32 [256], P('tp'), may hold values from 0.05 to 1.5
- state_in: bfloat16 [4096, 16], P('ctx'), may hold values from -6 to 6
- state_out: bfloat16 [4096, 16], P('ctx'), may hold values from -6 to 6
- skip_gain: float32 [256], P('tp'), may hold values from 0.5 to 1.5
- norm_gain: float32 [16384], P('tp'), may hold values from 0.5 to 1.5
Outputs:
- attn_out: bfloat16 [4096, 8192], P('ctx', 'tp')
- mamba_out: bfloat16 [4096, 16384], P('ctx', 'tp')
Inputs may be any that keep to these rules, and one draw needn't show every extreme that they name: `block_plan`: each row lists 4 distinct offsets, the first of them 0.
All inputs are finite; a program needn't handle non-finite values.
Results may differ from a plain program's by a relative error of at most 0.007.
Values may be sent and summed in bfloat16 or wider, within the bound.
A program may use at most 128 MiB of HBM per device.

v0:
```python
import functools
import math

import jax
import jax.numpy as jnp
from jax import lax
from jax.experimental import pallas as pl
from jax.experimental.pallas import tpu as pltpu
from jax.sharding import PartitionSpec as P


HEAD_WIDTH = 128
SPAN = 8
GROUP = 8
LANES = 128
NEG = -1e30


def from_behind(x, axis, by):
    size = lax.axis_size(axis)
    return lax.ppermute(x, axis, [(i, i + by) for i in range(size - by)])


def longest_reach(ctx):
    return min(ctx - 1, 4 if ctx <= SPAN else SPAN)


def pair_lanes(low, high, lane):
    return jnp.where(lane, low, high)


def split_state(state):
    high = state.astype(jnp.bfloat16)
    low = (state - high.astype(jnp.float32)).astype(jnp.bfloat16)
    return jnp.concatenate([high, low], axis=0)


def attention_kernel(width, pieces, active, start, q, *refs):
    keys, values = refs[: 2 * pieces : 2], refs[1 : 2 * pieces : 2]
    out, bias, acc, peak, total = refs[2 * pieces :]
    rows = q.shape[0]
    heads = q.shape[1] // width
    scale = width**-0.5 * math.log2(math.e)
    key_at = lax.broadcasted_iota(jnp.int32, (rows, rows), 0)
    query_at = lax.broadcasted_iota(jnp.int32, (rows, rows), 1)

    def fold(piece):
        seen = key_at - piece * rows >= start[...]
        if piece == 0:
            seen = seen & (key_at <= query_at)
        bias[...] = jnp.where(seen, 0.0, NEG)
        value_t = values[piece][...].T

        def one_head(h, _):
            at = pl.ds(pl.multiple_of(h * width, width), width)
            scores = lax.dot_general(
                keys[piece][...],
                q[:, at],
                (((1,), (1,)), ((), ())),
                preferred_element_type=jnp.float32,
            )
            scores = scores * scale + bias[...]
            top = jnp.max(scores, axis=0, keepdims=True)
            if piece > 0:
                top = jnp.maximum(top, peak[h])
            weights = jnp.exp2(scores - top)
            part = jnp.sum(weights, axis=0, keepdims=True)
            weighted = jnp.dot(
                value_t, weights.astype(jnp.bfloat16), preferred_element_type=jnp.float32
            )
            if piece > 0:
                factor = jnp.exp2(peak[h] - top)
                part = part + total[h] * factor
                weighted = weighted + acc[h] * factor
            peak[h] = top
            total[h] = part
            acc[h] = weighted
            return 0

        lax.fori_loop(0, heads, one_head, 0)

    fold(0)
    for piece in range(1, pieces):
        pl.when(active[piece] > 0)(functools.partial(fold, piece))

    def finish(h, _):
        at = pl.ds(pl.multiple_of(h * width, width), width)
        out[:, at] = (acc[h] / total[h]).T.astype(out.dtype)
        return 0

    lax.fori_loop(0, heads, finish, 0)


def attention(q, blocks, start, active, kv_heads):
    rows = q.shape[0]
    wide = q.shape[1] // kv_heads
    pieces = len(blocks)
    heads = wide // HEAD_WIDTH
    specs = [
        pl.BlockSpec((1, rows), lambda i, a: (0, 0)),
        pl.BlockSpec((rows, wide), lambda i, a: (0, i)),
    ]
    operands = [start, q]
    for key_rows, value_rows, first in blocks:
        specs.append(pl.BlockSpec((rows, HEAD_WIDTH), lambda i, a: (0, i)))
        specs.append(pl.BlockSpec((rows, HEAD_WIDTH), lambda i, a, first=first: (0, first + i)))
        operands += [key_rows, value_rows]
    return pl.pallas_call(
        functools.partial(attention_kernel, HEAD_WIDTH, pieces),
        out_shape=jax.ShapeDtypeStruct(q.shape, jnp.bfloat16),
        grid_spec=pltpu.PrefetchScalarGridSpec(
            num_scalar_prefetch=1,
            grid=(kv_heads,),
            in_specs=specs,
            out_specs=pl.BlockSpec((rows, wide), lambda i, a: (0, i)),
            scratch_shapes=[
                pltpu.VMEM((rows, rows), jnp.float32),
                pltpu.VMEM((heads, HEAD_WIDTH, rows), jnp.float32),
                pltpu.VMEM((heads, 1, rows), jnp.float32),
                pltpu.VMEM((heads, 1, rows), jnp.float32),
            ],
        ),
        cost_estimate=pl.CostEstimate(
            flops=8 * rows * rows * q.shape[1] * 2,
            bytes_accessed=4 * q.size,
            transcendentals=4 * rows * rows * kv_heads * heads,
        ),
        name="attend",
    )(active, *operands)


def scan_kernel(chunk, x, factors, rates_t, state_in, state_in_t, out_twice, start, skip, y, state, mix):
    rows = x.shape[0]
    chunks = rows // chunk
    states = state_in.shape[1]

    @pl.when(pl.program_id(0) == 0)
    def _():
        later = lax.broadcasted_iota(jnp.int32, (chunk, chunk), 0)
        earlier = lax.broadcasted_iota(jnp.int32, (chunk, chunk), 1)
        for c in range(chunks):
            at = pl.ds(c * chunk, chunk)
            both = lax.dot_general(
                out_twice[at, :states],
                state_in[at, :],
                (((1,), (1,)), ((), ())),
                preferred_element_type=jnp.float32,
            )
            seen = (later >= earlier) & (earlier + c * chunk >= start[at, :])
            mix[c] = jnp.where(seen, both, 0.0)

    lane = lax.broadcasted_iota(jnp.int32, (chunk, LANES), 1) < LANES // 2
    lane_row = lax.broadcasted_iota(jnp.int32, (1, LANES), 1) < LANES // 2
    for pair in range(GROUP // 2):
        cols = pl.ds(pair * LANES, LANES)
        a, b = 2 * pair, 2 * pair + 1
        held = None
        for c in range(chunks):
            at = pl.ds(c * chunk, chunk)

            def column(kind, h):
                return factors[0, at, pl.ds(kind * GROUP + h, 1)]

            def wide(kind):
                return pair_lanes(column(kind, a), column(kind, b), lane)

            values = x[at, cols].astype(jnp.float32)
            drive = (wide(3) * values).astype(jnp.bfloat16)

            def local(h):
                gap = jnp.minimum(column(0, h) - rates_t[pl.ds(h, 1), at], 0.0)
                mixing = (jnp.exp(gap) * mix[c]).astype(jnp.bfloat16)
                return jnp.dot(mixing, drive, preferred_element_type=jnp.float32)

            result = pair_lanes(local(a), local(b), lane) + skip[:, cols] * values
            tail = (wide(2) * drive.astype(jnp.float32)).astype(jnp.bfloat16)
            added = jnp.dot(state_in_t[:, at], tail, preferred_element_type=jnp.float32)
            if held is not None:
                result = result + wide(1) * jnp.dot(
                    out_twice[at, :], split_state(held), preferred_element_type=jnp.float32
                )
                last = pl.ds(c * chunk + chunk - 1, 1)
                kept = pair_lanes(
                    factors[0, last, pl.ds(GROUP + a, 1)],
                    factors[0, last, pl.ds(GROUP + b, 1)],
                    lane_row,
                )
                added = added + kept * held
            held = added
            y[at, cols] = result
        state[:, cols] = held


def local_scan(x, factors, rates_t, state_in, state_in_t, out_twice, start, skip, chunk):
    rows, channels = x.shape
    groups = factors.shape[0]
    wide = channels // groups
    states = state_in.shape[1]
    whole = lambda shape: pl.BlockSpec(shape, lambda i: (0, 0))
    return pl.pallas_call(
        functools.partial(scan_kernel, chunk),
        out_shape=(
            jax.ShapeDtypeStruct((rows, channels), jnp.float32),
            jax.ShapeDtypeStruct((states, channels), jnp.float32),
        ),
        grid=(groups,),
        in_specs=[
            pl.BlockSpec((rows, wide), lambda i: (0, i)),
            pl.BlockSpec((1,) + factors.shape[1:], lambda i: (i, 0, 0)),
            pl.BlockSpec((GROUP, rows), lambda i: (i, 0)),
            whole(state_in.shape),
            whole(state_in_t.shape),
            whole(out_twice.shape),
            whole(start.shape),
            pl.BlockSpec((1, wide), lambda i: (0, i)),
        ],
        out_specs=(
            pl.BlockSpec((rows, wide), lambda i: (0, i)),
            pl.BlockSpec((states, wide), lambda i: (0, i)),
        ),
        scratch_shapes=[pltpu.VMEM((rows // chunk, chunk, chunk), jnp.float32)],
        cost_estimate=pl.CostEstimate(
            flops=16 * rows * chunk * channels,
            bytes_accessed=8 * x.size,
            transcendentals=rows * chunk * groups * GROUP,
        ),
        name="local_scan",
    )(x, factors, rates_t, state_in, state_in_t, out_twice, start, skip)


def gate_kernel(y, gate, incoming, reach, out_twice, gated, squares):
    rows = y.shape[0]
    lane = lax.broadcasted_iota(jnp.int32, (rows, LANES), 1) < LANES // 2
    folded = jnp.zeros((rows, LANES), jnp.float32)
    for pair in range(GROUP // 2):
        cols = pl.ds(pair * LANES, LANES)
        wide = pair_lanes(
            reach[0, :, pl.ds(2 * pair, 1)], reach[0, :, pl.ds(2 * pair + 1, 1)], lane
        )
        carried = jnp.dot(
            out_twice[...], split_state(incoming[:, cols]), preferred_element_type=jnp.float32
        )
        g = gate[:, cols].astype(jnp.float32)
        value = (y[:, cols] + wide * carried) * (g / (1.0 + jnp.exp(-g)))
        gated[:, cols] = value
        folded = folded + value * value

    @pl.when(pl.program_id(0) == 0)
    def _():
        squares[...] = folded

    @pl.when(pl.program_id(0) > 0)
    def _():
        squares[...] += folded


def gate_all(y, gate, incoming, reach, out_twice):
    rows, channels = y.shape
    groups = reach.shape[0]
    wide = channels // groups
    return pl.pallas_call(
        gate_kernel,
        out_shape=(
            jax.ShapeDtypeStruct((rows, channels), jnp.float32),
            jax.ShapeDtypeStruct((rows, LANES), jnp.float32),
        ),
        grid=(groups,),
        in_specs=[
            pl.BlockSpec((rows, wide), lambda i: (0, i)),
            pl.BlockSpec((rows, wide), lambda i: (0, i)),
            pl.BlockSpec((incoming.shape[0], wide), lambda i: (0, i)),
            pl.BlockSpec((1,) + reach.shape[1:], lambda i: (i, 0, 0)),
            pl.BlockSpec(out_twice.shape, lambda i: (0, 0)),
        ],
        out_specs=(
            pl.BlockSpec((rows, wide), lambda i: (0, i)),
            pl.BlockSpec((rows, LANES), lambda i: (0, 0)),
        ),
        cost_estimate=pl.CostEstimate(
            flops=80 * y.size, bytes_accessed=10 * y.size, transcendentals=y.size
        ),
        name="gate_all",
    )(y, gate, incoming, reach, out_twice)


def layer(
    queries,
    keys,
    values,
    block_plan,
    doc_lengths,
    scan_input,
    gate_input,
    step_size,
    decay_rate,
    state_in,
    state_out,
    skip_gain,
    norm_gain,
):
    ctx, tp = lax.axis_size("ctx"), lax.axis_size("tp")
    me = lax.axis_index("ctx")
    rows = queries.shape[0]
    heads = decay_rate.shape[0]
    channels = scan_input.shape[1]
    head_dim = channels // heads
    groups = heads // GROUP
    kv_heads = keys.shape[1] // HEAD_WIDTH
    chunk = math.gcd(rows, 256)
    chunks = rows // chunk
    doc_reach = longest_reach(ctx)
    key_reach = min(doc_reach, SPAN - 1)

    window = jnp.concatenate([keys, values], axis=1)
    arrived = []
    for by in range(1, key_reach + 1):
        arrived.append(from_behind(window, "ctx", by))

    offsets = jnp.arange(rows, dtype=jnp.int32)
    positions = me * rows + offsets
    doc_ends = jnp.cumsum(doc_lengths)
    start = jnp.sum(
        jnp.where(doc_ends[None, :] <= positions[:, None], doc_lengths[None, :], 0), axis=1
    ).astype(jnp.int32) - me * rows

    step = step_size.astype(jnp.float32)
    rate = (-decay_rate[None, :] * step).reshape(chunks, chunk, heads)
    lower = jnp.tril(jnp.ones((chunk, chunk), jnp.float32))
    cumulative = jnp.einsum("ts,csh->cth", lower, rate, precision=lax.Precision.HIGHEST)
    start_chunks = start.reshape(chunks, chunk)
    first = jnp.arange(chunks, dtype=jnp.int32)[:, None] * chunk
    enters = jnp.where((start_chunks < first)[..., None], jnp.exp(cumulative), 0.0)
    in_tail = offsets.reshape(chunks, chunk) >= start_chunks[:, -1:]
    tails = jnp.where(in_tail[..., None], jnp.exp(cumulative[:, -1:] - cumulative), 0.0)
    through = jnp.ones((heads,), jnp.float32)
    reach = []
    for c in range(chunks):
        reach.append(enters[c] * through[None, :])
        through = through * enters[c, -1]
    reach = jnp.stack(reach).reshape(rows, groups, GROUP).transpose(1, 0, 2)
    flat = cumulative.reshape(rows, heads)
    factors = (
        jnp.stack([flat, enters.reshape(rows, heads), tails.reshape(rows, heads), step], axis=1)
        .reshape(rows, 4, groups, GROUP)
        .transpose(2, 0, 1, 3)
        .reshape(groups, rows, 4 * GROUP)
    )
    out_twice = jnp.concatenate([state_out, state_out], axis=1)
    skip = jnp.repeat(skip_gain, head_dim)[None, :]
    y, end_state = local_scan(
        scan_input,
        factors,
        flat.T,
        state_in,
        state_in.T,
        out_twice,
        start[:, None],
        skip,
        chunk,
    )

    states_n = state_in.shape[1]
    side = jnp.zeros((states_n, -(-heads // LANES) * LANES), jnp.float32).at[0, :heads].set(through)
    packed = jnp.concatenate([end_state, side], axis=1).astype(jnp.bfloat16)
    states = []
    for by in range(1, doc_reach + 1):
        states.append(from_behind(packed, "ctx", by))

    plan_row = lax.dynamic_index_in_dim(block_plan, me, 0, keepdims=False)
    back = jnp.arange(key_reach + 1, dtype=jnp.int32)
    active = (
        jnp.any(plan_row[None, :] == back[:, None], axis=1)
        & (me >= back)
        & (start[0] < -(back - 1) * rows)
    ).astype(jnp.int32)
    blocks = [(keys, values, 0)] + [(kv, kv, kv_heads) for kv in arrived]
    attn_out = attention(queries, blocks, start[None, :], active, kv_heads)

    incoming = states[-1][:, :channels].astype(jnp.float32)
    for state in states[-2::-1]:
        passed = state[0, channels : channels + heads].astype(jnp.float32)
        incoming = (
            state[:, :channels].astype(jnp.float32)
            + jnp.repeat(passed, head_dim)[None, :] * incoming
        )

    gated, squares = gate_all(y, gate_input, incoming, reach, out_twice)
    own = jnp.sum(squares, axis=1).reshape(-1, LANES)
    total = own
    for by in range(1, tp):
        total = total + lax.ppermute(own, "tp", [(i, (i + by) % tp) for i in range(tp)])
    mean = total.reshape(rows) / (channels * tp)
    mamba_out = (gated * lax.rsqrt(mean + 1e-05)[:, None] * norm_gain[None, :]).astype(jnp.bfloat16)
    return (attn_out, mamba_out)


def solution(mesh):
    in_specs = (
        P("ctx", "tp"),
        P("ctx", "tp"),
        P("ctx", "tp"),
        P(),
        P(),
        P("ctx", "tp"),
        P("ctx", "tp"),
        P("ctx", "tp"),
        P("tp"),
        P("ctx", None),
        P("ctx", None),
        P("tp"),
        P("tp"),
    )
    out_specs = (P("ctx", "tp"), P("ctx", "tp"))
    return jax.shard_map(layer, mesh=mesh, in_specs=in_specs, out_specs=out_specs, check_vma=False)
```

profile of v0, /device:TPU:28, one launch (start us, length us, event | category | flops | bytes accessed | tf_op | source)
XLA Modules:
  0.0 173.3 jit_solution(12978935659693003442)
XLA Ops:
  0.6 0.0 copy-start
  0.7 0.0 copy-start.6
  0.7 0.7 neg.8
  1.4 0.9 convert_multiply_fusion
  2.3 0.4 fusion.1
  2.7 0.2 slice_reduce_fusion
  2.8 0.1 copy.67
  3.0 0.9 convert_bitcast_fusion
  3.8 0.7 copy.65
  4.6 0.1 reduce.3
  4.7 0.7 select_reduce_fusion
  5.5 0.2 slice_reduce_fusion.2
  5.7 0.1 add_compare_fusion
  5.8 0.1 exponential_select_fusion.1
  5.9 0.1 copy.68
  6.0 0.2 fusion.10
  6.2 0.1 stack.17
  6.3 0.1 copy.69
  6.4 0.1 stack.18
  6.5 0.1 stack.16
  6.7 1.9 %copy.72.factors = f32[8,512,32]{2,1,0:T(8,128)} copy(f32[8,512,32]{1,2,0:T(8,128)S(1)} %copy_bitcast_fusion) | data formatting | bytes 1048576 | tf_op jit(solution)/shard_map/reshape | solution.py:346
  8.6 0.9 copy.75.start
  9.5 0.7 copy.80
  10.1 0.8 copy.74.out_twice
  10.9 0.7 copy.73.state_in
  11.6 0.1 broadcast_in_dim.70
  11.7 0.7 broadcast_in_dim_reshape.2.skip
  12.4 20.8 %local_scan.1 = (f32[512,4096]{1,0:T(8,128)}, f32[16,4096]{1,0:T(8,128)}) custom-call(bf16[512,4096]{1,0:T(8,128)(2,1)} %x.3, f32[8,512,32]{2,1,0:T(8,128)} %copy.72.factors, f32[64,512]{1,0:T(8,128)} %bitcast.60, bf16[512,16]{1,0:T(8,128)(2,1)} %copy.73.state_in, bf16[16,512]{1,0:T(8,128)(2,1)} %bitcast.63, bf16[512,32]{1,0:T(8,128)(2,1)} %copy.74.out_twice, ...), custom_call_target="tpu_custom_call" | custom-call | flops 8589934592 | bytes 16777216 | tf_op jit(solution)/shard_map/local_scan/pallas_call | solution.py:200
  33.2 1.0 convert.12
  34.2 1.3 collective-permute-start.6
  35.5 1.3 collective-permute-start.4
  36.8 1.3 collective-permute-start.5
  38.1 1.3 collective-permute-start.7
  39.5 1.3 collective-permute-start
  40.8 0.2 slice_reduce_fusion.1
  41.0 0.1 fusion.17
  41.1 0.5 slice.60
  41.6 0.1 copy.76
  41.8 0.1 reshape.218
  41.9 1.9 %copy.77 = f32[512,8,8]{2,0,1:T(8,128)} copy(f32[512,8,8]{0,2,1:T(8,128)S(1)} %reshape.218) | data formatting | bytes 262144 | tf_op jit(solution)/shard_map/reshape | solution.py:340
  43.8 0.2 dynamic-slice_reduce_fusion
  44.0 0.1 fusion.11
  44.1 1.3 collective-permute-start.1
  45.4 0.1 broadcast_in_dim.73
  45.5 0.1 mul.100
  45.5 0.1 broadcast_in_dim.71
  45.6 0.1 mul.96
  45.7 3.8 %collective-permute-done.5 = bf16[16,4224]{1,0:T(8,128)(2,1)S(1)} collective-permute-done((bf16[16,4224]{1,0:T(8,128)(2,1)S(1)}, bf16[16,4224]{1,0:T(8,128)(2,1)S(1)}, u32[]{:S(2)}, u32[]{:S(2)}) %collective-permute-start.5) | collective-permute-done | bytes 135200 | tf_op jit(solution)/shard_map/ppermute | solution.py:21
  49.5 0.1 broadcast_in_dim.72
  49.6 0.1 mul.98
  49.6 7.2 %collective-permute-done.7 = bf16[16,4224]{1,0:T(8,128)(2,1)S(1)} collective-permute-done((bf16[16,4224]{1,0:T(8,128)(2,1)S(1)}, bf16[16,4224]{1,0:T(8,128)(2,1)S(1)}, u32[]{:S(2)}, u32[]{:S(2)}) %collective-permute-start.7) | collective-permute-done | bytes 135200 | tf_op jit(solution)/shard_map/ppermute | solution.py:21
  56.9 0.8 multiply_add_fusion.incoming
  57.7 13.0 %gate_all.1 = (f32[512,4096]{1,0:T(8,128)}, f32[512,128]{1,0:T(8,128)}) custom-call(f32[512,4096]{1,0:T(8,128)} %get-tuple-element.18.y, bf16[512,4096]{1,0:T(8,128)(2,1)} %gate.1, f32[16,4096]{1,0:T(8,128)} %multiply_add_fusion.incoming, f32[8,512,8]{2,1,0:T(8,128)} %bitcast.55, bf16[512,32]{1,0:T(8,128)(2,1)} %copy.74.out_twice), custom_call_target="tpu_custom_call" | custom-call | flops 167772160 | bytes 20971520 | tf_op jit(solution)/shard_map/gate_all/pallas_call | solution.py:261
  70.6 1.1 reduce_sum.19
  71.7 1.1 collective-permute-start.10
  72.8 1.0 collective-permute-start.9
  73.8 1.1 and_convert_fusion.active
  74.9 1.3 collective-permute-start.2
  76.2 1.5 collective-permute-start.3
  77.7 6.7 %multiply_convert_fusion = bf16[512,4096]{1,0:T(8,128)(2,1)} fusion(f32[512,4096]{1,0:T(8,128)} %get-tuple-element.20, f32[4096]{0:T(1024)S(1)} %copy-done.4, f32[512]{0:T(512)S(1)} %rsqrt_bitcast_fusion), kind=kLoop, calls=%fused_computation | loop fusion | flops 6291456 | bytes 12601344 | tf_op jit(solution)/shard_map/convert_element_type | solution.py:393
  84.5 9.7 %collective-permute-done.2.refs_6_.refs_7_ = bf16[512,512]{1,0:T(8,128)(2,1)S(1)} collective-permute-done((bf16[512,512]{1,0:T(8,128)(2,1)S(1)}, bf16[512,512]{1,0:T(8,128)(2,1)S(1)}, u32[]{:S(2)}, u32[]{:S(2)}) %collective-permute-start.2) | collective-permute-done | bytes 524320 | tf_op jit(solution)/shard_map/ppermute | solution.py:21
  94.2 29.9 %collective-permute-done.3.refs_8_.refs_9_ = bf16[512,512]{1,0:T(8,128)(2,1)S(1)} collective-permute-done((bf16[512,512]{1,0:T(8,128)(2,1)S(1)}, bf16[512,512]{1,0:T(8,128)(2,1)S(1)}, u32[]{:S(2)}, u32[]{:S(2)}) %collective-permute-start.3) | collective-permute-done | bytes 524320 | tf_op jit(solution)/shard_map/ppermute | solution.py:21
  124.2 0.8 copy-done.11
  125.0 48.3 %attend.1 = bf16[512,2048]{1,0:T(8,128)(2,1)} custom-call(s32[5]{0:T(128)} %and_convert_fusion.active, s32[1,512]{1,0:T(1,128)} %bitcast.62, bf16[512,2048]{1,0:T(8,128)(2,1)} %q.1, bf16[512,256]{1,0:T(8,128)(2,1)} %refs_0_.1, bf16[512,256]{1,0:T(8,128)(2,1)} %refs_1_.1, bf16[512,512]{1,0:T(8,128)(2,1)} %copy-done.8, bf16[512,512]{1,0:T(8,128)(2,1)} %copy-done.8, ...), custom_call_target="tpu_custom_call" | custom-call | flops 8589934592 | bytes 4194304 | tf_op jit(solution)/shard_map/attend/pallas_call | solution.py:108
  (44 shorter events, 0.3 us)
Async XLA Ops:
  0.6 43.2 %copy-start = (s32[8,4]{0,1:T(4,128)S(1)}, s32[8,4]{0,1:T(4,128)}, u32[]{:S(2)}) copy-start(s32[8,4]{0,1:T(4,128)} %param.18) | copy-start | bytes 388
  0.6 9.5 %copy-start.5 = (bf16[512,16]{0,1:T(8,128)(2,1)S(1)}, bf16[512,16]{0,1:T(8,128)(2,1)}, u32[]{:S(2)}) copy-start(bf16[512,16]{0,1:T(8,128)(2,1)} %param.25) | copy-start | bytes 49156
  0.7 10.2 %copy-start.6 = (bf16[512,16]{0,1:T(8,128)(2,1)S(1)}, bf16[512,16]{0,1:T(8,128)(2,1)}, u32[]{:S(2)}) copy-start(bf16[512,16]{0,1:T(8,128)(2,1)} %param.24) | copy-start | bytes 49156
  0.7 11.0 %copy-start.7 = (f32[64]{0:T(128)S(1)}, f32[64]{0:T(128)}, u32[]{:S(2)}) copy-start(f32[64]{0:T(128)} %param.26) | copy-start | bytes 772
  5.5 35.6 %copy-start.3 = (s32[512]{0:T(512)}, s32[512]{0:T(512)S(1)}, u32[]{:S(2)}) copy-start(s32[512]{0:T(512)S(1)} %broadcast_subtract_fusion) | copy-start | bytes 6148
  12.4 27.0 %copy-start.1 = (bf16[512,256]{1,0:T(8,128)(2,1)S(1)}, bf16[512,256]{1,0:T(8,128)(2,1)}, u32[]{:S(2)}) copy-start(bf16[512,256]{1,0:T(8,128)(2,1)} %refs_0_.1) | copy-start | bytes 786436
  12.4 27.1 %copy-start.2 = (bf16[512,256]{1,0:T(8,128)(2,1)S(1)}, bf16[512,256]{1,0:T(8,128)(2,1)}, u32[]{:S(2)}) copy-start(bf16[512,256]{1,0:T(8,128)(2,1)} %refs_1_.1) | copy-start | bytes 786436
  34.2 9.8 %collective-permute-start.6 = (bf16[16,4224]{1,0:T(8,128)(2,1)S(1)}, bf16[16,4224]{1,0:T(8,128)(2,1)S(1)}, u32[]{:S(2)}, u32[]{:S(2)}) collective-permute-start(bf16[16,4224]{1,0:T(8,128)(2,1)S(1)} %fusion.4), channel_id=1, source_target_pairs={{0,12},{4,16},{8,20},{12,24},{16,28},{1,13},{5,17},{9,21},{13,25},... | collective-permute-start | bytes 405512 | tf_op jit(solution)/shard_map/ppermute | solution.py:21
  35.5 10.0 %collective-permute-start.4 = (bf16[16,4224]{1,0:T(8,128)(2,1)S(1)}, bf16[16,4224]{1,0:T(8,128)(2,1)S(1)}, u32[]{:S(2)}, u32[]{:S(2)}) collective-permute-start(bf16[16,4224]{1,0:T(8,128)(2,1)S(1)} %fusion.4), channel_id=1, source_target_pairs={{0,4},{4,8},{8,12},{12,16},{16,20},{20,24},{24,28},{1,5},{5,9},{9,... | collective-permute-start | bytes 405512 | tf_op jit(solution)/shard_map/ppermute | solution.py:21
  36.8 12.6 %collective-permute-start.5 = (bf16[16,4224]{1,0:T(8,128)(2,1)S(1)}, bf16[16,4224]{1,0:T(8,128)(2,1)S(1)}, u32[]{:S(2)}, u32[]{:S(2)}) collective-permute-start(bf16[16,4224]{1,0:T(8,128)(2,1)S(1)} %fusion.4), channel_id=1, source_target_pairs={{0,8},{4,12},{8,16},{12,20},{16,24},{20,28},{1,9},{5,13},{9,17},{1... | collective-permute-start | bytes 405512 | tf_op jit(solution)/shard_map/ppermute | solution.py:21
  38.1 18.7 %collective-permute-start.7 = (bf16[16,4224]{1,0:T(8,128)(2,1)S(1)}, bf16[16,4224]{1,0:T(8,128)(2,1)S(1)}, u32[]{:S(2)}, u32[]{:S(2)}) collective-permute-start(bf16[16,4224]{1,0:T(8,128)(2,1)S(1)} %fusion.4), channel_id=1, source_target_pairs={{0,16},{4,20},{8,24},{12,28},{1,17},{5,21},{9,25},{13,29},{2,18},{... | collective-permute-start | bytes 405512 | tf_op jit(solution)/shard_map/ppermute | solution.py:21
  39.5 45.0 %collective-permute-start = (bf16[512,512]{1,0:T(8,128)(2,1)S(1)}, bf16[512,512]{1,0:T(8,128)(2,1)S(1)}, u32[]{:S(2)}, u32[]{:S(2)}) collective-permute-start(bf16[512,512]{1,0:T(8,128)(2,1)S(1)} %constant_dynamic-update-slice_fusion), channel_id=1, source_target_pairs={{0,4},{4,8},{8,12},{12,16},{16,20},{20,24},{24,28},{1,5},{5,9},{9,... | collective-permute-start | bytes 1572872 | tf_op jit(solution)/shard_map/ppermute | solution.py:21
  44.1 40.4 %collective-permute-start.1 = (bf16[512,512]{1,0:T(8,128)(2,1)S(1)}, bf16[512,512]{1,0:T(8,128)(2,1)S(1)}, u32[]{:S(2)}, u32[]{:S(2)}) collective-permute-start(bf16[512,512]{1,0:T(8,128)(2,1)S(1)} %constant_dynamic-update-slice_fusion), channel_id=1, source_target_pairs={{0,8},{4,12},{8,16},{12,20},{16,24},{20,28},{1,9},{5,13},{9,17},{1... | collective-permute-start | bytes 1572872 | tf_op jit(solution)/shard_map/ppermute | solution.py:21
  57.7 20.1 %copy-start.4 = (f32[4096]{0:T(1024)S(1)}, f32[4096]{0:T(1024)}, u32[]{:S(2)}) copy-start(f32[4096]{0:T(1024)} %param.27) | copy-start | bytes 49156
  71.7 3.2 %collective-permute-start.10 = (f32[4,128]{1,0:T(4,128)S(1)}, f32[4,128]{1,0:T(4,128)S(1)}, u32[]{:S(2)}, u32[]{:S(2)}) collective-permute-start(f32[4,128]{1,0:T(4,128)S(1)} %bitcast.64), channel_id=1, source_target_pairs={{0,3},{1,0},{2,1},{3,2},{4,7},{5,4},{6,5},{7,6},{8,11},{9,8},{10,9... | collective-permute-start | bytes 6152 | tf_op jit(solution)/shard_map/ppermute | solution.py:391
  72.8 3.4 %collective-permute-start.8 = (f32[4,128]{1,0:T(4,128)S(1)}, f32[4,128]{1,0:T(4,128)S(1)}, u32[]{:S(2)}, u32[]{:S(2)}) collective-permute-start(f32[4,128]{1,0:T(4,128)S(1)} %bitcast.65), channel_id=1, source_target_pairs={{0,1},{1,2},{2,3},{3,0},{4,5},{5,6},{6,7},{7,4},{8,9},{9,10},{10,1... | collective-permute-start | bytes 6152 | tf_op jit(solution)/shard_map/ppermute | solution.py:391
  72.8 4.9 %collective-permute-start.9 = (f32[4,128]{1,0:T(4,128)S(1)}, f32[4,128]{1,0:T(4,128)S(1)}, u32[]{:S(2)}, u32[]{:S(2)}) collective-permute-start(f32[4,128]{1,0:T(4,128)S(1)} %bitcast.66), channel_id=1, source_target_pairs={{0,2},{1,3},{2,0},{3,1},{4,6},{5,7},{6,4},{7,5},{8,10},{9,11},{10,... | collective-permute-start | bytes 6152 | tf_op jit(solution)/shard_map/ppermute | solution.py:391
  74.9 19.3 %collective-permute-start.2 = (bf16[512,512]{1,0:T(8,128)(2,1)S(1)}, bf16[512,512]{1,0:T(8,128)(2,1)S(1)}, u32[]{:S(2)}, u32[]{:S(2)}) collective-permute-start(bf16[512,512]{1,0:T(8,128)(2,1)S(1)} %constant_dynamic-update-slice_fusion), channel_id=1, source_target_pairs={{0,12},{4,16},{8,20},{12,24},{16,28},{1,13},{5,17},{9,21},{13,25},... | collective-permute-start | bytes 1572872 | tf_op jit(solution)/shard_map/ppermute | solution.py:21
  76.2 48.0 %collective-permute-start.3 = (bf16[512,512]{1,0:T(8,128)(2,1)S(1)}, bf16[512,512]{1,0:T(8,128)(2,1)S(1)}, u32[]{:S(2)}, u32[]{:S(2)}) collective-permute-start(bf16[512,512]{1,0:T(8,128)(2,1)S(1)} %constant_dynamic-update-slice_fusion), channel_id=1, source_target_pairs={{0,16},{4,20},{8,24},{12,28},{1,17},{5,21},{9,25},{13,29},{2,18},{... | collective-permute-start | bytes 1572872 | tf_op jit(solution)/shard_map/ppermute | solution.py:21
  84.5 39.7 %copy-start.8 = (bf16[512,512]{1,0:T(8,128)(2,1)}, bf16[512,512]{1,0:T(8,128)(2,1)S(1)}, u32[]{:S(2)}) copy-start(bf16[512,512]{1,0:T(8,128)(2,1)S(1)} %collective-permute-done.refs_2_.refs_3_) | copy-start | bytes 1572868
  84.5 39.7 %copy-start.9 = (bf16[512,512]{1,0:T(8,128)(2,1)}, bf16[512,512]{1,0:T(8,128)(2,1)S(1)}, u32[]{:S(2)}) copy-start(bf16[512,512]{1,0:T(8,128)(2,1)S(1)} %collective-permute-done.1.refs_4_.refs_5_) | copy-start | bytes 1572868
  94.2 30.0 %copy-start.10 = (bf16[512,512]{1,0:T(8,128)(2,1)}, bf16[512,512]{1,0:T(8,128)(2,1)S(1)}, u32[]{:S(2)}) copy-start(bf16[512,512]{1,0:T(8,128)(2,1)S(1)} %collective-permute-done.2.refs_6_.refs_7_) | copy-start | bytes 1572868
  124.2 0.8 copy-start.11
where the time goes:
time: 174 us; the launch traced here: 173 us
  Pallas kernels  82.1 us (47%)
  waiting for transfers between devices  50.7 us (29%)
  other arithmetic  14.7 us (8%)
  starting transfers between devices  12.5 us (7%)
  local copies, waits for them, and re-layouts  11.8 us (7%)
    ppermute x8, waiting for transfers between devices, from_behind(): return lax.ppermute(x, axis, [(i, i + by) for i in range(size - by)])  50.7 us
    pallas_call x1, Pallas kernels, attention(): pl.pallas_call(functools.partial(attention_kernel, HEAD_WIDTH, pieces), o...  48.3 us
    pallas_call x1, Pallas kernels, local_scan(): pl.pallas_call(functools.partial(scan_kernel, chunk), out_shape=(jax.Shap...  20.8 us
    pallas_call x1, Pallas kernels, gate_all(): pl.pallas_call(gate_kernel, out_shape=(jax.ShapeDtypeStruct((rows, channe...  13 us
    ppermute x8, starting transfers between devices, from_behind(): return lax.ppermute(x, axis, [(i, i + by) for i in range(size - by)])  10.5 us
    convert_element_type x1, other arithmetic, layer(): (gated * lax.rsqrt(mean + 1e-05)[:, None] * norm_gain[None, :]).astype(jn...  6.74 us
  transfers between devices with their start and end apart: 11, of which 4 were waited for; matrix products, arithmetic and copies ran while one was open for 8% of the time, Pallas kernels for 7%

commit v1 on v0

--- a/solution.py
+++ b/solution.py
@@ -35,52 +35,79 @@
     return jnp.concatenate([high, low], axis=0)
 
 
-def attention_kernel(width, pieces, active, start, q, *refs):
-    keys, values = refs[: 2 * pieces : 2], refs[1 : 2 * pieces : 2]
-    out, bias, acc, peak, total = refs[2 * pieces :]
+def fold_head(width, keys, value_t, queries, bias, before):
+    scale = width**-0.5 * math.log2(math.e)
+    scores = lax.dot_general(
+        keys, queries, (((1,), (1,)), ((), ())), preferred_element_type=jnp.float32
+    )
+    scores = scores * scale + bias
+    top = jnp.max(scores, axis=0, keepdims=True)
+    if before is not None:
+        top = jnp.maximum(top, before[0])
+    weights = jnp.exp2(scores - top)
+    part = jnp.sum(weights, axis=0, keepdims=True)
+    weighted = jnp.dot(value_t, weights.astype(jnp.bfloat16), preferred_element_type=jnp.float32)
+    if before is not None:
+        factor = jnp.exp2(before[0] - top)
+        part = part + before[1] * factor
+        weighted = weighted + before[2] * factor
+    return top, part, weighted
+
+
+def own_kernel(width, start, q, keys, values, peak, total, acc, bias):
     rows = q.shape[0]
     heads = q.shape[1] // width
-    scale = width**-0.5 * math.log2(math.e)
+    half = rows // 2
     key_at = lax.broadcasted_iota(jnp.int32, (rows, rows), 0)
     query_at = lax.broadcasted_iota(jnp.int32, (rows, rows), 1)
+    bias[...] = jnp.where((key_at >= start[...]) & (key_at <= query_at), 0.0, NEG)
+    value_t = values[...].T
+
+    def one_head(h, _):
+        at = pl.ds(pl.multiple_of(h * width, width), width)
+        for lo in (0, half):
+            seen = lo + half
+            cols = pl.ds(lo, half)
+            top, part, weighted = fold_head(
+                width, keys[:seen, :], value_t[:, :seen], q[cols, at], bias[:seen, cols], None
+            )
+            peak[h, :, cols] = top
+            total[h, :, cols] = part
+            acc[h, :, cols] = weighted
+        return 0
+
+    lax.fori_loop(0, heads, one_head, 0, unroll=2)
+
+
+def attention_kernel(width, pieces, active, start, q, peak_in, total_in, acc_in, *refs):
+    keys, values = refs[: 2 * pieces : 2], refs[1 : 2 * pieces : 2]
+    out, bias, peak, total, acc = refs[2 * pieces :]
+    rows = q.shape[0]
+    heads = q.shape[1] // width
+    key_at = lax.broadcasted_iota(jnp.int32, (rows, rows), 0)
+    peak[...] = peak_in[...]
+    total[...] = total_in[...]
+    acc[...] = acc_in[...]
 
     def fold(piece):
-        seen = key_at - piece * rows >= start[...]
-        if piece == 0:
-            seen = seen & (key_at <= query_at)
-        bias[...] = jnp.where(seen, 0.0, NEG)
+        bias[...] = jnp.where(key_at - (piece + 1) * rows >= start[...], 0.0, NEG)
         value_t = values[piece][...].T
 
         def one_head(h, _):
             at = pl.ds(pl.multiple_of(h * width, width), width)
-            scores = lax.dot_general(
+            peak[h], total[h], acc[h] = fold_head(
+                width,
                 keys[piece][...],
+                value_t,
                 q[:, at],
-                (((1,), (1,)), ((), ())),
-                preferred_element_type=jnp.float32,
+                bias[...],
+                (peak[h], total[h], acc[h]),
             )
-            scores = scores * scale + bias[...]
-            top = jnp.max(scores, axis=0, keepdims=True)
-            if piece > 0:
-                top = jnp.maximum(top, peak[h])
-            weights = jnp.exp2(scores - top)
-            part = jnp.sum(weights, axis=0, keepdims=True)
-            weighted = jnp.dot(
-                value_t, weights.astype(jnp.bfloat16), preferred_element_type=jnp.float32
-            )
-            if piece > 0:
-                factor = jnp.exp2(peak[h] - top)
-                part = part + total[h] * factor
-                weighted = weighted + acc[h] * factor
-            peak[h] = top
-            total[h] = part
-            acc[h] = weighted
             return 0
 
-        lax.fori_loop(0, heads, one_head, 0)
-
-    fold(0)
-    for piece in range(1, pieces):
+        lax.fori_loop(0, heads, one_head, 0, unroll=2)
+
+    for piece in range(pieces):
         pl.when(active[piece] > 0)(functools.partial(fold, piece))
 
     def finish(h, _):
@@ -91,7 +118,43 @@
     lax.fori_loop(0, heads, finish, 0)
 
 
-def attention(q, blocks, start, active, kv_heads):
+def attention_sums(rows, heads, kv_heads):
+    shapes = [(heads, 1, rows), (heads, 1, rows), (heads, HEAD_WIDTH, rows)]
+    specs = [pl.BlockSpec((heads // kv_heads,) + s[1:], lambda i, *a: (i, 0, 0)) for s in shapes]
+    return [jax.ShapeDtypeStruct(s, jnp.float32) for s in shapes], specs
+
+
+def attend_cost(q, blocks):
+    return pl.CostEstimate(
+        flops=4 * blocks * q.shape[0] * q.size,
+        bytes_accessed=8 * q.size,
+        transcendentals=blocks * q.shape[0] * q.size // HEAD_WIDTH,
+    )
+
+
+def own_attention(q, keys, values, start, kv_heads):
+    rows = q.shape[0]
+    wide = q.shape[1] // kv_heads
+    shapes, specs = attention_sums(rows, q.shape[1] // HEAD_WIDTH, kv_heads)
+    by_head = pl.BlockSpec((rows, HEAD_WIDTH), lambda i: (0, i))
+    return pl.pallas_call(
+        functools.partial(own_kernel, HEAD_WIDTH),
+        out_shape=shapes,
+        grid=(kv_heads,),
+        in_specs=[
+            pl.BlockSpec((1, rows), lambda i: (0, 0)),
+            pl.BlockSpec((rows, wide), lambda i: (0, i)),
+            by_head,
+            by_head,
+        ],
+        out_specs=specs,
+        scratch_shapes=[pltpu.VMEM((rows, rows), jnp.float32)],
+        cost_estimate=attend_cost(q, 1),
+        name="attend_own",
+    )(start, q, keys, values)
+
+
+def attention(q, sums, blocks, start, active, kv_heads):
     rows = q.shape[0]
     wide = q.shape[1] // kv_heads
     pieces = len(blocks)
@@ -99,12 +162,12 @@
     specs = [
         pl.BlockSpec((1, rows), lambda i, a: (0, 0)),
         pl.BlockSpec((rows, wide), lambda i, a: (0, i)),
-    ]
-    operands = [start, q]
-    for key_rows, value_rows, first in blocks:
+    ] + attention_sums(rows, q.shape[1] // HEAD_WIDTH, kv_heads)[1]
+    operands = [start, q, *sums]
+    for block in blocks:
         specs.append(pl.BlockSpec((rows, HEAD_WIDTH), lambda i, a: (0, i)))
-        specs.append(pl.BlockSpec((rows, HEAD_WIDTH), lambda i, a, first=first: (0, first + i)))
-        operands += [key_rows, value_rows]
+        specs.append(pl.BlockSpec((rows, HEAD_WIDTH), lambda i, a: (0, kv_heads + i)))
+        operands += [block, block]
     return pl.pallas_call(
         functools.partial(attention_kernel, HEAD_WIDTH, pieces),
         out_shape=jax.ShapeDtypeStruct(q.shape, jnp.bfloat16),
@@ -115,16 +178,12 @@
             out_specs=pl.BlockSpec((rows, wide), lambda i, a: (0, i)),
             scratch_shapes=[
                 pltpu.VMEM((rows, rows), jnp.float32),
-                pltpu.VMEM((heads, HEAD_WIDTH, rows), jnp.float32),
                 pltpu.VMEM((heads, 1, rows), jnp.float32),
                 pltpu.VMEM((heads, 1, rows), jnp.float32),
+                pltpu.VMEM((heads, HEAD_WIDTH, rows), jnp.float32),
             ],
         ),
-        cost_estimate=pl.CostEstimate(
-            flops=8 * rows * rows * q.shape[1] * 2,
-            bytes_accessed=4 * q.size,
-            transcendentals=4 * rows * rows * kv_heads * heads,
-        ),
+        cost_estimate=attend_cost(q, 3),
         name="attend",
     )(active, *operands)
 
@@ -187,7 +246,7 @@
                 )
                 added = added + kept * held
             held = added
-            y[at, cols] = result
+            y[at, cols] = result.astype(y.dtype)
         state[:, cols] = held
 
 
@@ -200,7 +259,7 @@
     return pl.pallas_call(
         functools.partial(scan_kernel, chunk),
         out_shape=(
-            jax.ShapeDtypeStruct((rows, channels), jnp.float32),
+            jax.ShapeDtypeStruct((rows, channels), jnp.bfloat16),
             jax.ShapeDtypeStruct((states, channels), jnp.float32),
         ),
         grid=(groups,),
@@ -241,8 +300,8 @@
             out_twice[...], split_state(incoming[:, cols]), preferred_element_type=jnp.float32
         )
         g = gate[:, cols].astype(jnp.float32)
-        value = (y[:, cols] + wide * carried) * (g / (1.0 + jnp.exp(-g)))
-        gated[:, cols] = value
+        value = (y[:, cols].astype(jnp.float32) + wide * carried) * (g / (1.0 + jnp.exp(-g)))
+        gated[:, cols] = value.astype(gated.dtype)
         folded = folded + value * value
 
     @pl.when(pl.program_id(0) == 0)
@@ -261,7 +320,7 @@
     return pl.pallas_call(
         gate_kernel,
         out_shape=(
-            jax.ShapeDtypeStruct((rows, channels), jnp.float32),
+            jax.ShapeDtypeStruct((rows, channels), jnp.bfloat16),
             jax.ShapeDtypeStruct((rows, LANES), jnp.float32),
         ),
         grid=(groups,),
@@ -367,14 +426,14 @@
         states.append(from_behind(packed, "ctx", by))
 
     plan_row = lax.dynamic_index_in_dim(block_plan, me, 0, keepdims=False)
-    back = jnp.arange(key_reach + 1, dtype=jnp.int32)
+    back = jnp.arange(1, key_reach + 1, dtype=jnp.int32)
     active = (
         jnp.any(plan_row[None, :] == back[:, None], axis=1)
         & (me >= back)
         & (start[0] < -(back - 1) * rows)
     ).astype(jnp.int32)
-    blocks = [(keys, values, 0)] + [(kv, kv, kv_heads) for kv in arrived]
-    attn_out = attention(queries, blocks, start[None, :], active, kv_heads)
+    sums = own_attention(queries, keys, values, start[None, :], kv_heads)
+    attn_out = attention(queries, sums, arrived, start[None, :], active, kv_heads)
 
     incoming = states[-1][:, :channels].astype(jnp.float32)
     for state in states[-2::-1]:
@@ -390,7 +449,7 @@
     for by in range(1, tp):
         total = total + lax.ppermute(own, "tp", [(i, (i + by) % tp) for i in range(tp)])
     mean = total.reshape(rows) / (channels * tp)
-    mamba_out = (gated * lax.rsqrt(mean + 1e-05)[:, None] * norm_gain[None, :]).astype(jnp.bfloat16)
+    mamba_out = (gated.astype(jnp.float32) * lax.rsqrt(mean + 1e-05)[:, None] * norm_gain[None, :]).astype(jnp.bfloat16)
     return (attn_out, mamba_out)
 
 

time: 174 us -> 168 us (0.966)
  waiting for transfers between devices: 50.7 us -> 47.7 us
  Pallas kernels: 82.1 us -> 79.5 us
    pallas_call x1, Pallas kernels: 48.3 us -> 34.3 us  [attention(): pl.pallas_call(functools.partial(attention_kernel, HEAD_WIDTH, pieces), o...]
    pallas_call x0 -> x1, Pallas kernels: none -> 13.5 us  [own_attention(): pl.pallas_call(functools.partial(own_kernel, HEAD_WIDTH), out_shape=shape...]
    ppermute x8, waiting for transfers between devices: 50.7 us -> 47.7 us  [from_behind(): return lax.ppermute(x, axis, [(i, i + by) for i in range(size - by)])]
    pallas_call x1, Pallas kernels: 13 us -> 11 us  [gate_all(): pl.pallas_call(gate_kernel, out_shape=(jax.ShapeDtypeStruct((rows, channe...]
  transfers between devices with their start and end apart: 11 -> 11, of which waited for: 4 -> 4; matrix products, arithmetic and copies ran while one was open for 8% -> 8% of each run, Pallas kernels for 7% -> 15%
where the time goes in v1:
time: 168 us; the launch traced here: 167 us
  Pallas kernels  79.5 us (47%)
  waiting for transfers between devices  47.7 us (28%)
  other arithmetic  14 us (8%)
  starting transfers between devices  12.5 us (7%)
  local copies, waits for them, and re-layouts  11.9 us (7%)
    ppermute x8, waiting for transfers between devices, from_behind(): return lax.ppermute(x, axis, [(i, i + by) for i in range(size - by)])  47.7 us
    pallas_call x1, Pallas kernels, attention(): pl.pallas_call(functools.partial(attention_kernel, HEAD_WIDTH, pieces), o...  34.3 us
    pallas_call x1, Pallas kernels, local_scan(): pl.pallas_call(functools.partial(scan_kernel, chunk), out_shape=(jax.Shap...  20.6 us
    pallas_call x1, Pallas kernels, own_attention(): pl.pallas_call(functools.partial(own_kernel, HEAD_WIDTH), out_shape=shape...  13.5 us
    pallas_call x1, Pallas kernels, gate_all(): pl.pallas_call(gate_kernel, out_shape=(jax.ShapeDtypeStruct((rows, channe...  11 us
    ppermute x8, starting transfers between devices, from_behind(): return lax.ppermute(x, axis, [(i, i + by) for i in range(size - by)])  10.5 us
    convert_element_type x1, other arithmetic, layer(): (gated.astype(jnp.float32) * lax.rsqrt(mean + 1e-05)[:, None] * norm_gain...  5.84 us
  transfers between devices with their start and end apart: 11, of which 4 were waited for; matrix products, arithmetic and copies ran while one was open for 8% of the time, Pallas kernels for 15%

profile of v1, /device:TPU:28, one launch (start us, length us, event | category | flops | bytes accessed | tf_op | source)
XLA Modules:
  0.0 167.1 jit_solution(12444059856266093960)
XLA Ops:
  0.6 0.0 copy-start
  0.7 0.7 neg.8
  1.4 0.9 convert_multiply_fusion
  2.3 0.4 fusion.1
  2.7 0.2 slice_reduce_fusion
  2.8 0.1 copy.67
  3.0 0.9 convert_bitcast_fusion
  3.8 0.7 copy.65
  4.6 0.1 reduce.3
  4.7 0.7 select_reduce_fusion
  5.5 0.2 slice_reduce_fusion.2
  5.7 0.1 add_compare_fusion
  5.8 0.1 exponential_select_fusion.1
  5.9 0.1 copy.68
  6.0 0.2 fusion.10
  6.2 0.1 stack.17
  6.3 0.1 copy.69
  6.4 0.1 stack.18
  6.5 0.1 stack.16
  6.7 1.9 %copy.72.factors = f32[8,512,32]{2,1,0:T(8,128)} copy(f32[8,512,32]{1,2,0:T(8,128)S(1)} %copy_bitcast_fusion) | data formatting | bytes 1048576 | tf_op jit(solution)/shard_map/reshape | solution.py:405
  8.6 0.8 copy.75.start
  9.4 0.6 copy.80
  10.1 0.8 copy.74.out_twice
  10.9 0.8 copy.73.state_in
  11.6 0.1 broadcast_in_dim.71
  11.7 0.7 broadcast_in_dim_reshape.2.skip
  12.4 20.6 %local_scan.1 = (bf16[512,4096]{1,0:T(8,128)(2,1)}, f32[16,4096]{1,0:T(8,128)}) custom-call(bf16[512,4096]{1,0:T(8,128)(2,1)} %x.3, f32[8,512,32]{2,1,0:T(8,128)} %copy.72.factors, f32[64,512]{1,0:T(8,128)} %bitcast.60, bf16[512,16]{1,0:T(8,128)(2,1)} %copy.73.state_in, bf16[16,512]{1,0:T(8,128)(2,1)} %bitcast.64, bf16[512,32]{1,0:T(8,128)(2,1)} %copy.74.out_twice, ...), custom_call_target="tpu_custom_call" | custom-call | flops 8589934592 | bytes 16777216 | tf_op jit(solution)/shard_map/local_scan/pallas_call | solution.py:259
  33.0 1.0 convert.12
  34.0 1.3 collective-permute-start.6
  35.3 1.3 collective-permute-start.4
  36.6 1.3 collective-permute-start.5
  37.9 1.3 collective-permute-start.7
  39.3 1.3 collective-permute-start
  40.6 0.2 slice_reduce_fusion.1
  40.8 0.6 slice.60
  41.3 0.1 fusion.16
  41.4 0.1 copy.76
  41.5 0.1 reshape.222
  41.7 1.9 %copy.77 = f32[512,8,8]{2,0,1:T(8,128)} copy(f32[512,8,8]{0,2,1:T(8,128)S(1)} %reshape.222) | data formatting | bytes 262144 | tf_op jit(solution)/shard_map/reshape | solution.py:399
  43.6 0.2 dynamic-slice_reduce_fusion
  43.8 0.2 compare_reduce_fusion
  44.0 1.3 and_convert_fusion.active
  45.2 1.3 collective-permute-start.1
  46.5 0.1 broadcast_in_dim.74
  46.6 0.1 mul.100
  46.7 0.1 broadcast_in_dim.72
  46.8 0.1 mul.96
  46.9 2.4 %collective-permute-done.5 = bf16[16,4224]{1,0:T(8,128)(2,1)S(1)} collective-permute-done((bf16[16,4224]{1,0:T(8,128)(2,1)S(1)}, bf16[16,4224]{1,0:T(8,128)(2,1)S(1)}, u32[]{:S(2)}, u32[]{:S(2)}) %collective-permute-start.5) | collective-permute-done | bytes 135200 | tf_op jit(solution)/shard_map/ppermute | solution.py:21
  49.2 0.1 broadcast_in_dim.73
  49.3 0.1 mul.98
  49.4 7.2 %collective-permute-done.7 = bf16[16,4224]{1,0:T(8,128)(2,1)S(1)} collective-permute-done((bf16[16,4224]{1,0:T(8,128)(2,1)S(1)}, bf16[16,4224]{1,0:T(8,128)(2,1)S(1)}, u32[]{:S(2)}, u32[]{:S(2)}) %collective-permute-start.7) | collective-permute-done | bytes 135200 | tf_op jit(solution)/shard_map/ppermute | solution.py:21
  56.6 0.8 multiply_add_fusion.incoming
  57.4 11.0 %gate_all.1 = (bf16[512,4096]{1,0:T(8,128)(2,1)}, f32[512,128]{1,0:T(8,128)}) custom-call(bf16[512,4096]{1,0:T(8,128)(2,1)} %get-tuple-element.24.y, bf16[512,4096]{1,0:T(8,128)(2,1)} %gate.1, f32[16,4096]{1,0:T(8,128)} %multiply_add_fusion.incoming, f32[8,512,8]{2,1,0:T(8,128)} %bitcast.55, bf16[512,32]{1,0:T(8,128)(2,1)} %copy.74.out_twice), custom_call_target="tpu_custom_call" | custom-call | flops 167772160 | bytes 20971520 | tf_op jit(solution)/shard_map/gate_all/pallas_call | solution.py:320
  68.4 1.1 reduce_sum.19
  69.5 1.1 collective-permute-start.10
  70.6 1.0 collective-permute-start.9
  71.6 13.5 %attend_own.1 = (f32[16,1,512]{2,1,0:T(1,128)}, f32[16,1,512]{2,1,0:T(1,128)}, f32[16,128,512]{2,1,0:T(8,128)}) custom-call(s32[1,512]{1,0:T(1,128)} %bitcast.62, bf16[512,2048]{1,0:T(8,128)(2,1)} %q.3, bf16[512,256]{1,0:T(8,128)(2,1)} %keys.1, bf16[512,256]{1,0:T(8,128)(2,1)} %values.1), custom_call_target="tpu_custom_call" | custom-call | flops 2147483648 | bytes 8388608 | tf_op jit(solution)/shard_map/attend_own/pallas_call | solution.py:140
  85.1 1.3 collective-permute-start.2
  86.4 1.5 collective-permute-start.3
  87.9 5.8 %multiply_convert_fusion = bf16[512,4096]{1,0:T(8,128)(2,1)} fusion(bf16[512,4096]{1,0:T(8,128)(2,1)} %get-tuple-element.26, f32[4096]{0:T(1024)S(1)} %copy-done.4, f32[512]{0:T(512)S(1)} %rsqrt_bitcast_fusion), kind=kLoop, calls=%fused_computation | loop fusion | flops 8388608 | bytes 8407040 | tf_op jit(solution)/shard_map/convert_element_type | solution.py:452
  93.8 10.6 %collective-permute-done.2.refs_4_.refs_5_ = bf16[512,512]{1,0:T(8,128)(2,1)S(1)} collective-permute-done((bf16[512,512]{1,0:T(8,128)(2,1)S(1)}, bf16[512,512]{1,0:T(8,128)(2,1)S(1)}, u32[]{:S(2)}, u32[]{:S(2)}) %collective-permute-start.2) | collective-permute-done | bytes 524320 | tf_op jit(solution)/shard_map/ppermute | solution.py:21
  104.4 27.4 %collective-permute-done.3.refs_6_.refs_7_ = bf16[512,512]{1,0:T(8,128)(2,1)S(1)} collective-permute-done((bf16[512,512]{1,0:T(8,128)(2,1)S(1)}, bf16[512,512]{1,0:T(8,128)(2,1)S(1)}, u32[]{:S(2)}, u32[]{:S(2)}) %collective-permute-start.3) | collective-permute-done | bytes 524320 | tf_op jit(solution)/shard_map/ppermute | solution.py:21
  131.8 0.8 copy-done.11
  132.6 34.3 %attend.1 = bf16[512,2048]{1,0:T(8,128)(2,1)} custom-call(s32[4]{0:T(128)} %and_convert_fusion.active, s32[1,512]{1,0:T(1,128)} %bitcast.63, bf16[512,2048]{1,0:T(8,128)(2,1)} %q.3, f32[16,1,512]{2,1,0:T(1,128)} %get-tuple-element.21.peak_in, f32[16,1,512]{2,1,0:T(1,128)} %get-tuple-element.22.total_in, f32[16,128,512]{2,1,0:T(8,128)} %get-tuple-element.23.acc_in, ...), custom_call_target="tpu_custom_call" | custom-call | flops 6442450944 | bytes 8388608 | tf_op jit(solution)/shard_map/attend/pallas_call | solution.py:171
  (46 shorter events, 0.3 us)
Async XLA Ops:
  0.6 43.0 %copy-start = (s32[8,4]{0,1:T(4,128)S(1)}, s32[8,4]{0,1:T(4,128)}, u32[]{:S(2)}) copy-start(s32[8,4]{0,1:T(4,128)} %param.18) | copy-start | bytes 388
  0.6 9.4 %copy-start.5 = (bf16[512,16]{0,1:T(8,128)(2,1)S(1)}, bf16[512,16]{0,1:T(8,128)(2,1)}, u32[]{:S(2)}) copy-start(bf16[512,16]{0,1:T(8,128)(2,1)} %param.25) | copy-start | bytes 49156
  0.7 10.2 %copy-start.6 = (bf16[512,16]{0,1:T(8,128)(2,1)S(1)}, bf16[512,16]{0,1:T(8,128)(2,1)}, u32[]{:S(2)}) copy-start(bf16[512,16]{0,1:T(8,128)(2,1)} %param.24) | copy-start | bytes 49156
  0.7 10.9 %copy-start.7 = (f32[64]{0:T(128)S(1)}, f32[64]{0:T(128)}, u32[]{:S(2)}) copy-start(f32[64]{0:T(128)} %param.26) | copy-start | bytes 772
  5.5 35.3 %copy-start.3 = (s32[512]{0:T(512)}, s32[512]{0:T(512)S(1)}, u32[]{:S(2)}) copy-start(s32[512]{0:T(512)S(1)} %broadcast_subtract_fusion) | copy-start | bytes 6148
  12.4 26.8 %copy-start.1 = (bf16[512,256]{1,0:T(8,128)(2,1)S(1)}, bf16[512,256]{1,0:T(8,128)(2,1)}, u32[]{:S(2)}) copy-start(bf16[512,256]{1,0:T(8,128)(2,1)} %keys.1) | copy-start | bytes 786436
  12.4 26.9 %copy-start.2 = (bf16[512,256]{1,0:T(8,128)(2,1)S(1)}, bf16[512,256]{1,0:T(8,128)(2,1)}, u32[]{:S(2)}) copy-start(bf16[512,256]{1,0:T(8,128)(2,1)} %values.1) | copy-start | bytes 786436
  34.0 11.3 %collective-permute-start.6 = (bf16[16,4224]{1,0:T(8,128)(2,1)S(1)}, bf16[16,4224]{1,0:T(8,128)(2,1)S(1)}, u32[]{:S(2)}, u32[]{:S(2)}) collective-permute-start(bf16[16,4224]{1,0:T(8,128)(2,1)S(1)} %fusion.4), channel_id=1, source_target_pairs={{0,12},{4,16},{8,20},{12,24},{16,28},{1,13},{5,17},{9,21},{13,25},... | collective-permute-start | bytes 405512 | tf_op jit(solution)/shard_map/ppermute | solution.py:21
  35.3 11.4 %collective-permute-start.4 = (bf16[16,4224]{1,0:T(8,128)(2,1)S(1)}, bf16[16,4224]{1,0:T(8,128)(2,1)S(1)}, u32[]{:S(2)}, u32[]{:S(2)}) collective-permute-start(bf16[16,4224]{1,0:T(8,128)(2,1)S(1)} %fusion.4), channel_id=1, source_target_pairs={{0,4},{4,8},{8,12},{12,16},{16,20},{20,24},{24,28},{1,5},{5,9},{9,... | collective-permute-start | bytes 405512 | tf_op jit(solution)/shard_map/ppermute | solution.py:21
  36.6 12.6 %collective-permute-start.5 = (bf16[16,4224]{1,0:T(8,128)(2,1)S(1)}, bf16[16,4224]{1,0:T(8,128)(2,1)S(1)}, u32[]{:S(2)}, u32[]{:S(2)}) collective-permute-start(bf16[16,4224]{1,0:T(8,128)(2,1)S(1)} %fusion.4), channel_id=1, source_target_pairs={{0,8},{4,12},{8,16},{12,20},{16,24},{20,28},{1,9},{5,13},{9,17},{1... | collective-permute-start | bytes 405512 | tf_op jit(solution)/shard_map/ppermute | solution.py:21
  37.9 18.7 %collective-permute-start.7 = (bf16[16,4224]{1,0:T(8,128)(2,1)S(1)}, bf16[16,4224]{1,0:T(8,128)(2,1)S(1)}, u32[]{:S(2)}, u32[]{:S(2)}) collective-permute-start(bf16[16,4224]{1,0:T(8,128)(2,1)S(1)} %fusion.4), channel_id=1, source_target_pairs={{0,16},{4,20},{8,24},{12,28},{1,17},{5,21},{9,25},{13,29},{2,18},{... | collective-permute-start | bytes 405512 | tf_op jit(solution)/shard_map/ppermute | solution.py:21
  39.3 54.5 %collective-permute-start = (bf16[512,512]{1,0:T(8,128)(2,1)S(1)}, bf16[512,512]{1,0:T(8,128)(2,1)S(1)}, u32[]{:S(2)}, u32[]{:S(2)}) collective-permute-start(bf16[512,512]{1,0:T(8,128)(2,1)S(1)} %constant_dynamic-update-slice_fusion), channel_id=1, source_target_pairs={{0,4},{4,8},{8,12},{12,16},{16,20},{20,24},{24,28},{1,5},{5,9},{9,... | collective-permute-start | bytes 1572872 | tf_op jit(solution)/shard_map/ppermute | solution.py:21
  45.2 48.5 %collective-permute-start.1 = (bf16[512,512]{1,0:T(8,128)(2,1)S(1)}, bf16[512,512]{1,0:T(8,128)(2,1)S(1)}, u32[]{:S(2)}, u32[]{:S(2)}) collective-permute-start(bf16[512,512]{1,0:T(8,128)(2,1)S(1)} %constant_dynamic-update-slice_fusion), channel_id=1, source_target_pairs={{0,8},{4,12},{8,16},{12,20},{16,24},{20,28},{1,9},{5,13},{9,17},{1... | collective-permute-start | bytes 1572872 | tf_op jit(solution)/shard_map/ppermute | solution.py:21
  68.4 19.5 %copy-start.4 = (f32[4096]{0:T(1024)S(1)}, f32[4096]{0:T(1024)}, u32[]{:S(2)}) copy-start(f32[4096]{0:T(1024)} %param.27) | copy-start | bytes 49156
  69.5 15.6 %collective-permute-start.10 = (f32[4,128]{1,0:T(4,128)S(1)}, f32[4,128]{1,0:T(4,128)S(1)}, u32[]{:S(2)}, u32[]{:S(2)}) collective-permute-start(f32[4,128]{1,0:T(4,128)S(1)} %bitcast.65), channel_id=1, source_target_pairs={{0,3},{1,0},{2,1},{3,2},{4,7},{5,4},{6,5},{7,6},{8,11},{9,8},{10,9... | collective-permute-start | bytes 6152 | tf_op jit(solution)/shard_map/ppermute | solution.py:450
  70.6 15.8 %collective-permute-start.8 = (f32[4,128]{1,0:T(4,128)S(1)}, f32[4,128]{1,0:T(4,128)S(1)}, u32[]{:S(2)}, u32[]{:S(2)}) collective-permute-start(f32[4,128]{1,0:T(4,128)S(1)} %bitcast.66), channel_id=1, source_target_pairs={{0,1},{1,2},{2,3},{3,0},{4,5},{5,6},{6,7},{7,4},{8,9},{9,10},{10,1... | collective-permute-start | bytes 6152 | tf_op jit(solution)/shard_map/ppermute | solution.py:450
  70.6 17.3 %collective-permute-start.9 = (f32[4,128]{1,0:T(4,128)S(1)}, f32[4,128]{1,0:T(4,128)S(1)}, u32[]{:S(2)}, u32[]{:S(2)}) collective-permute-start(f32[4,128]{1,0:T(4,128)S(1)} %bitcast.67), channel_id=1, source_target_pairs={{0,2},{1,3},{2,0},{3,1},{4,6},{5,7},{6,4},{7,5},{8,10},{9,11},{10,... | collective-permute-start | bytes 6152 | tf_op jit(solution)/shard_map/ppermute | solution.py:450
  85.1 19.3 %collective-permute-start.2 = (bf16[512,512]{1,0:T(8,128)(2,1)S(1)}, bf16[512,512]{1,0:T(8,128)(2,1)S(1)}, u32[]{:S(2)}, u32[]{:S(2)}) collective-permute-start(bf16[512,512]{1,0:T(8,128)(2,1)S(1)} %constant_dynamic-update-slice_fusion), channel_id=1, source_target_pairs={{0,12},{4,16},{8,20},{12,24},{16,28},{1,13},{5,17},{9,21},{13,25},... | collective-permute-start | bytes 1572872 | tf_op jit(solution)/shard_map/ppermute | solution.py:21
  86.4 45.4 %collective-permute-start.3 = (bf16[512,512]{1,0:T(8,128)(2,1)S(1)}, bf16[512,512]{1,0:T(8,128)(2,1)S(1)}, u32[]{:S(2)}, u32[]{:S(2)}) collective-permute-start(bf16[512,512]{1,0:T(8,128)(2,1)S(1)} %constant_dynamic-update-slice_fusion), channel_id=1, source_target_pairs={{0,16},{4,20},{8,24},{12,28},{1,17},{5,21},{9,25},{13,29},{2,18},{... | collective-permute-start | bytes 1572872 | tf_op jit(solution)/shard_map/ppermute | solution.py:21
  93.8 38.1 %copy-start.8 = (bf16[512,512]{1,0:T(8,128)(2,1)}, bf16[512,512]{1,0:T(8,128)(2,1)S(1)}, u32[]{:S(2)}) copy-start(bf16[512,512]{1,0:T(8,128)(2,1)S(1)} %collective-permute-done.refs_0_.refs_1_) | copy-start | bytes 1572868
  93.8 38.1 %copy-start.9 = (bf16[512,512]{1,0:T(8,128)(2,1)}, bf16[512,512]{1,0:T(8,128)(2,1)S(1)}, u32[]{:S(2)}) copy-start(bf16[512,512]{1,0:T(8,128)(2,1)S(1)} %collective-permute-done.1.refs_2_.refs_3_) | copy-start | bytes 1572868
  104.4 27.5 %copy-start.10 = (bf16[512,512]{1,0:T(8,128)(2,1)}, bf16[512,512]{1,0:T(8,128)(2,1)S(1)}, u32[]{:S(2)}) copy-start(bf16[512,512]{1,0:T(8,128)(2,1)S(1)} %collective-permute-done.2.refs_4_.refs_5_) | copy-start | bytes 1572868
  131.8 0.8 copy-start.11
